TPU v7x, 512 devices: a whole 4x8x8 slice. The times are simulated.
512 devices in a mesh: occ: 8 (over z), vir: 64 (over y, x, core).
Axes of the slice: x: 4, y: 8, z: 8, core: 2. Of those that a mesh axis runs over, the one named last changes fastest.
Arguments:
- amplitudes: bfloat16 [6144, 2048], P('occ', 'vir'), may hold values from -6 to 6
- integrals: bfloat16 [2048, 163840], P('occ', 'vir'), may hold values from -0.375 to 0.375
- occ_sym: int32 [48], P('occ'), may hold values from 0 to 7, as said below
- vir_sym: int32 [1280], P('vir'), may hold values from 0 to 7, as said below
- k_sym: int32 [16], replicated, may hold values from 0 to 7
Outputs:
- ladder: bfloat16 [6144, 163840], P('occ', 'vir')
Inputs may be any that keep to these rules, and one draw needn't show every extreme that they name: `occ_sym`: among the 6 blocks of one index of occ no irrep occurs more than 2 times, and one occurs exactly 2 times. `vir_sym`: among the 20 blocks of one index of vir no irrep occurs more than 5 times, and one occurs exactly 5 times.
All inputs are finite; a program needn't handle non-finite values.
Results may differ from a plain program's by a relative error of at most 0.001.
Values may be sent and summed in bfloat16 or wider, within the bound.
A program may use at most 64 MiB of HBM per device.

v0:
```python
import jax
import jax.numpy as jnp
from jax import lax
from jax.sharding import PartitionSpec as P

BLK = 128
MAXB = 5


def slot_order(symmetry, labels, slot_bound):
    label_count = labels.shape[0]
    positions = jnp.arange(label_count, dtype=jnp.int32)
    matching = labels == symmetry
    ranking = jnp.where(matching, positions, positions + label_count)
    chosen = jnp.argsort(ranking)[:slot_bound]
    return (chosen, matching[chosen])


def slot_table(symmetry, labels, slot_bound):
    chosen, usable = slot_order(symmetry, labels, slot_bound)
    positions = jnp.arange(labels.shape[0], dtype=jnp.int32)
    return ((chosen[:, None] == positions[None, :]) & usable[:, None]).astype(jnp.bfloat16)


def per_device(amplitudes, integrals, occ_sym, vir_sym, k_sym):
    occ_rows = amplitudes.shape[0]
    occ_blocks = occ_rows // BLK
    kblocks = k_sym.shape[0]
    window = kblocks * BLK
    vir_blocks = vir_sym.shape[0]
    col_width = vir_blocks * BLK
    block_ids = jnp.arange(kblocks, dtype=jnp.int32)

    def column_table(symmetry):
        return slot_table(symmetry, vir_sym, MAXB)

    gathered = lax.all_gather(amplitudes, "vir", axis=1, tiled=True)
    allowed = (occ_sym[:, None] == k_sym[None, :]).astype(jnp.bfloat16)
    amp_masked = (
        gathered.reshape(occ_blocks, BLK, kblocks, BLK) * allowed[:, None, :, None]
    ).reshape(occ_rows, window)
    shard_rows = integrals.shape[0]
    own_count = shard_rows // BLK
    first_block = lax.axis_index("occ") * own_count
    own_ids = first_block + jnp.arange(own_count, dtype=jnp.int32)
    own_syms = jnp.sum(jnp.where(own_ids[:, None] == block_ids[None, :], k_sym[None, :], 0), axis=1)
    start_sum = jnp.zeros((occ_rows, vir_blocks, BLK), jnp.float32)
    tables_v = jax.vmap(column_table)(own_syms)
    packed_v = jnp.einsum(
        "bmv,brvc->brmc",
        tables_v,
        integrals.reshape(own_count, BLK, vir_blocks, BLK),
        preferred_element_type=jnp.float32,
    )
    packed_v = packed_v.astype(jnp.bfloat16).reshape(shard_rows, MAXB * BLK)
    shard_piece = lax.all_gather(packed_v, "occ", axis=0, tiled=True)
    piece_blocks = shard_piece.shape[0] // BLK

    def one_block(block_index, running_sum):
        row_start = block_index * BLK
        symmetry = jnp.sum(jnp.where(block_ids == row_start // BLK, k_sym, 0))
        chosen = slot_order(symmetry, vir_sym, MAXB)[0]
        amp_cols = lax.dynamic_slice_in_dim(amp_masked, row_start, BLK, 1)
        block_part = lax.dynamic_slice_in_dim(shard_piece, block_index * BLK, BLK, 0)
        product = jnp.dot(amp_cols, block_part, preferred_element_type=jnp.float32)
        return running_sum.at[:, chosen, :].add(product.reshape(occ_rows, MAXB, BLK))

    summed = lax.fori_loop(0, piece_blocks, one_block, start_sum)
    return summed.reshape(occ_rows, col_width).astype(jnp.bfloat16)


def solution(mesh):
    return jax.shard_map(
        per_device,
        mesh=mesh,
        in_specs=(P("occ", "vir"), P("occ", "vir"), P("occ"), P("vir"), P()),
        out_specs=P("occ", "vir"),
        check_vma=False,
    )
```

profile of v0, /device:TPU:4, one launch (start us, length us, event | category | flops | bytes accessed | tf_op | source)
XLA Modules:
  0.0 402.5 jit_solution(3272119504203592197)
XLA Ops:
  10.9 2.6 reshape.82
  15.0 82.5 %all-gather.3.cloned.1.call-done = bf16[768,2048]{0,1:T(8,128)(2,1)} async-done(((bf16[768,32]{0,1:T(8,128)(2,1)}), bf16[768,2048]{0,1:T(8,128)(2,1)}) %all-gather.3.cloned.1.call-update) | async-done | bytes 3145744 | tf_op jit(solution)/shard_map/all_gather | solution.py:37
  97.5 3.2 copy.43
  101.2 2.4 bitcast_multiply_fusion
  103.5 49.2 %all-gather.5.cloned.1.call-done = bf16[2048,640]{0,1:T(8,128)(2,1)} async-done(((bf16[256,640]{0,1:T(8,128)(2,1)}), bf16[2048,640]{0,1:T(8,128)(2,1)}) %all-gather.5.cloned.1.call-update) | async-done | bytes 2621456 | tf_op jit(solution)/shard_map/all_gather | solution.py:56
  152.7 3.9 broadcast_in_dim.62
  156.6 225.5 %while.16 = (s32[]{:T(128)}, f32[768,20,128]{2,0,1:T(8,128)}, s32[16]{0:T(128)S(1)}, s32[20]{0:T(128)S(1)}, bf16[768,2048]{1,0:T(8,128)(2,1)}, /*index=5*/bf16[2...) while((s32[]{:T(128)}, f32[768,20,128]{2,0,1:T(8,128)}, ...), condition=%wide.region_6.7_spmd.clone, body=%wide.region_2.6_spmd.clone.sunk | while | flops 126320880 | bytes 12158960 | solution.py:68
  158.0 1.7 sort.51
  159.7 2.7 fusion.23
  162.4 1.9 copy.63
  164.3 6.4 %scatter_fusion = f32[768,20,128]{2,0,1:T(8,128)} fusion(f32[768,20,128]{2,0,1:T(8,128)} %get-tuple-element.294, s32[5]{0:T(128)S(1)} %compare_select_fusion.8, f32[5,768,128]{2,1,0:T(8,128)S(1)} %bitcast.27), kind=kCustom, calls=%fused_computation.1.clone.clone.1 | custom fusion | flops 491520 | bytes 5898260 | tf_op jit(solution)/shard_map/while/body/eval_jaxpr/scatter-add | solution.py:66
  172.1 1.7 sort.51
  173.8 2.7 fusion.23
  176.4 1.9 copy.63
  178.3 6.4 %scatter_fusion = f32[768,20,128]{2,0,1:T(8,128)} fusion(f32[768,20,128]{2,0,1:T(8,128)} %get-tuple-element.294, s32[5]{0:T(128)S(1)} %compare_select_fusion.8, f32[5,768,128]{2,1,0:T(8,128)S(1)} %bitcast.27), kind=kCustom, calls=%fused_computation.1.clone.clone.1 | custom fusion | flops 491520 | bytes 5898260 | tf_op jit(solution)/shard_map/while/body/eval_jaxpr/scatter-add | solution.py:66
  187.8 2.7 fusion.23
  190.5 1.9 copy.63
  192.4 6.4 %scatter_fusion = f32[768,20,128]{2,0,1:T(8,128)} fusion(f32[768,20,128]{2,0,1:T(8,128)} %get-tuple-element.294, s32[5]{0:T(128)S(1)} %compare_select_fusion.8, f32[5,768,128]{2,1,0:T(8,128)S(1)} %bitcast.27), kind=kCustom, calls=%fused_computation.1.clone.clone.1 | custom fusion | flops 491520 | bytes 5898260 | tf_op jit(solution)/shard_map/while/body/eval_jaxpr/scatter-add | solution.py:66
  200.2 1.7 sort.51
  201.9 2.7 fusion.23
  204.6 1.9 copy.63
  206.5 6.4 %scatter_fusion = f32[768,20,128]{2,0,1:T(8,128)} fusion(f32[768,20,128]{2,0,1:T(8,128)} %get-tuple-element.294, s32[5]{0:T(128)S(1)} %compare_select_fusion.8, f32[5,768,128]{2,1,0:T(8,128)S(1)} %bitcast.27), kind=kCustom, calls=%fused_computation.1.clone.clone.1 | custom fusion | flops 491520 | bytes 5898260 | tf_op jit(solution)/shard_map/while/body/eval_jaxpr/scatter-add | solution.py:66
  214.3 1.7 sort.51
  216.0 2.7 fusion.23
  218.7 1.9 copy.63
  220.6 6.4 %scatter_fusion = f32[768,20,128]{2,0,1:T(8,128)} fusion(f32[768,20,128]{2,0,1:T(8,128)} %get-tuple-element.294, s32[5]{0:T(128)S(1)} %compare_select_fusion.8, f32[5,768,128]{2,1,0:T(8,128)S(1)} %bitcast.27), kind=kCustom, calls=%fused_computation.1.clone.clone.1 | custom fusion | flops 491520 | bytes 5898260 | tf_op jit(solution)/shard_map/while/body/eval_jaxpr/scatter-add | solution.py:66
  230.1 2.7 fusion.23
  232.7 1.9 copy.63
  234.6 6.4 %scatter_fusion = f32[768,20,128]{2,0,1:T(8,128)} fusion(f32[768,20,128]{2,0,1:T(8,128)} %get-tuple-element.294, s32[5]{0:T(128)S(1)} %compare_select_fusion.8, f32[5,768,128]{2,1,0:T(8,128)S(1)} %bitcast.27), kind=kCustom, calls=%fused_computation.1.clone.clone.1 | custom fusion | flops 491520 | bytes 5898260 | tf_op jit(solution)/shard_map/while/body/eval_jaxpr/scatter-add | solution.py:66
  242.5 1.7 sort.51
  244.1 2.7 fusion.23
  246.8 1.9 copy.63
  248.7 6.5 %scatter_fusion = f32[768,20,128]{2,0,1:T(8,128)} fusion(f32[768,20,128]{2,0,1:T(8,128)} %get-tuple-element.294, s32[5]{0:T(128)S(1)} %compare_select_fusion.8, f32[5,768,128]{2,1,0:T(8,128)S(1)} %bitcast.27), kind=kCustom, calls=%fused_computation.1.clone.clone.1 | custom fusion | flops 491520 | bytes 5898260 | tf_op jit(solution)/shard_map/while/body/eval_jaxpr/scatter-add | solution.py:66
  258.3 2.7 fusion.23
  261.0 1.9 copy.63
  262.8 6.4 %scatter_fusion = f32[768,20,128]{2,0,1:T(8,128)} fusion(f32[768,20,128]{2,0,1:T(8,128)} %get-tuple-element.294, s32[5]{0:T(128)S(1)} %compare_select_fusion.8, f32[5,768,128]{2,1,0:T(8,128)S(1)} %bitcast.27), kind=kCustom, calls=%fused_computation.1.clone.clone.1 | custom fusion | flops 491520 | bytes 5898260 | tf_op jit(solution)/shard_map/while/body/eval_jaxpr/scatter-add | solution.py:66
  270.7 1.7 sort.51
  272.3 2.7 fusion.23
  275.0 1.9 copy.63
  276.9 6.4 %scatter_fusion = f32[768,20,128]{2,0,1:T(8,128)} fusion(f32[768,20,128]{2,0,1:T(8,128)} %get-tuple-element.294, s32[5]{0:T(128)S(1)} %compare_select_fusion.8, f32[5,768,128]{2,1,0:T(8,128)S(1)} %bitcast.27), kind=kCustom, calls=%fused_computation.1.clone.clone.1 | custom fusion | flops 491520 | bytes 5898260 | tf_op jit(solution)/shard_map/while/body/eval_jaxpr/scatter-add | solution.py:66
  286.4 2.7 fusion.23
  289.1 1.9 copy.63
  291.0 6.5 %scatter_fusion = f32[768,20,128]{2,0,1:T(8,128)} fusion(f32[768,20,128]{2,0,1:T(8,128)} %get-tuple-element.294, s32[5]{0:T(128)S(1)} %compare_select_fusion.8, f32[5,768,128]{2,1,0:T(8,128)S(1)} %bitcast.27), kind=kCustom, calls=%fused_computation.1.clone.clone.1 | custom fusion | flops 491520 | bytes 5898260 | tf_op jit(solution)/shard_map/while/body/eval_jaxpr/scatter-add | solution.py:66
  300.6 2.7 fusion.23
  303.3 1.9 copy.63
  305.2 6.4 %scatter_fusion = f32[768,20,128]{2,0,1:T(8,128)} fusion(f32[768,20,128]{2,0,1:T(8,128)} %get-tuple-element.294, s32[5]{0:T(128)S(1)} %compare_select_fusion.8, f32[5,768,128]{2,1,0:T(8,128)S(1)} %bitcast.27), kind=kCustom, calls=%fused_computation.1.clone.clone.1 | custom fusion | flops 491520 | bytes 5898260 | tf_op jit(solution)/shard_map/while/body/eval_jaxpr/scatter-add | solution.py:66
  313.0 1.7 sort.51
  314.6 2.7 fusion.23
  317.3 1.9 copy.63
  319.2 6.5 %scatter_fusion = f32[768,20,128]{2,0,1:T(8,128)} fusion(f32[768,20,128]{2,0,1:T(8,128)} %get-tuple-element.294, s32[5]{0:T(128)S(1)} %compare_select_fusion.8, f32[5,768,128]{2,1,0:T(8,128)S(1)} %bitcast.27), kind=kCustom, calls=%fused_computation.1.clone.clone.1 | custom fusion | flops 491520 | bytes 5898260 | tf_op jit(solution)/shard_map/while/body/eval_jaxpr/scatter-add | solution.py:66
  328.7 2.7 fusion.23
  331.4 1.9 copy.63
  333.3 6.5 %scatter_fusion = f32[768,20,128]{2,0,1:T(8,128)} fusion(f32[768,20,128]{2,0,1:T(8,128)} %get-tuple-element.294, s32[5]{0:T(128)S(1)} %compare_select_fusion.8, f32[5,768,128]{2,1,0:T(8,128)S(1)} %bitcast.27), kind=kCustom, calls=%fused_computation.1.clone.clone.1 | custom fusion | flops 491520 | bytes 5898260 | tf_op jit(solution)/shard_map/while/body/eval_jaxpr/scatter-add | solution.py:66
  342.9 2.7 fusion.23
  345.6 1.9 copy.63
  347.5 6.5 %scatter_fusion = f32[768,20,128]{2,0,1:T(8,128)} fusion(f32[768,20,128]{2,0,1:T(8,128)} %get-tuple-element.294, s32[5]{0:T(128)S(1)} %compare_select_fusion.8, f32[5,768,128]{2,1,0:T(8,128)S(1)} %bitcast.27), kind=kCustom, calls=%fused_computation.1.clone.clone.1 | custom fusion | flops 491520 | bytes 5898260 | tf_op jit(solution)/shard_map/while/body/eval_jaxpr/scatter-add | solution.py:66
  357.0 2.7 fusion.23
  359.7 1.9 copy.63
  361.6 6.4 %scatter_fusion = f32[768,20,128]{2,0,1:T(8,128)} fusion(f32[768,20,128]{2,0,1:T(8,128)} %get-tuple-element.294, s32[5]{0:T(128)S(1)} %compare_select_fusion.8, f32[5,768,128]{2,1,0:T(8,128)S(1)} %bitcast.27), kind=kCustom, calls=%fused_computation.1.clone.clone.1 | custom fusion | flops 491520 | bytes 5898260 | tf_op jit(solution)/shard_map/while/body/eval_jaxpr/scatter-add | solution.py:66
  371.1 2.7 fusion.23
  373.8 1.9 copy.63
  375.7 6.5 %scatter_fusion = f32[768,20,128]{2,0,1:T(8,128)} fusion(f32[768,20,128]{2,0,1:T(8,128)} %get-tuple-element.294, s32[5]{0:T(128)S(1)} %compare_select_fusion.8, f32[5,768,128]{2,1,0:T(8,128)S(1)} %bitcast.27), kind=kCustom, calls=%fused_computation.1.clone.clone.1 | custom fusion | flops 491520 | bytes 5898260 | tf_op jit(solution)/shard_map/while/body/eval_jaxpr/scatter-add | solution.py:66
  382.2 7.2 %copy.51 = bf16[768,20,128]{0,2,1:T(8,128)(2,1)} copy(f32[768,20,128]{2,0,1:T(8,128)} %get-tuple-element.185) | data formatting | bytes 11796480 | tf_op jit(solution)/shard_map/while | solution.py:68
  389.4 6.3 %copy.52 = bf16[768,2560]{1,0:T(8,128)(2,1)} copy(bf16[768,2560]{0,1:T(8,128)(2,1)} %bitcast.29) | data formatting | bytes 7864320 | tf_op jit(solution)/shard_map/convert_element_type | solution.py:69
  (102 shorter events, 43.2 us)
Async XLA Ops:
  6.5 90.9 %all-gather.3.cloned.1.call-start = ((), (), s32[]{:S(2)}) async-start(), calls=%async_computation | async-start | bytes 3194880 | tf_op jit(solution)/shard_map/all_gather | solution.py:37
  7.3 145.4 %all-gather.5.cloned.1.call-start = ((), (), s32[]{:S(2)}) async-start(), calls=%async_computation.1 | async-start | bytes 2949120 | tf_op jit(solution)/shard_map/all_gather | solution.py:56
  10.9 4.0 copy-start
  10.9 4.0 copy-start.1
  103.5 53.1 %copy-start.2 = (s32[20]{0:T(128)S(1)}, s32[20]{0:T(128)}, u32[]{:S(2)}) copy-start(s32[20]{0:T(128)} %param.10) | copy-start | bytes 244
Sparse Core Ops, SparseCore 0:
  10.7 86.7 all-gather.2
  99.5 53.1 all-gather.4
where the time goes:
time: 405 us; the launch traced here: 402 us
  other arithmetic  157 us (39%)
  waiting for transfers between devices  132 us (33%)
  local copies, waits for them, and re-layouts  56 us (14%)
  matrix products  43.5 us (11%)
  between operations  13.5 us (3%)
    scatter-add x16, other arithmetic, one_block(): running_sum.at[:, chosen, :].add(product.reshape(occ_rows, MAXB, BLK))  103 us
    all_gather x1, waiting for transfers between devices, per_device(): gathered = lax.all_gather(amplitudes, 'vir', axis=1, tiled=True)  82.5 us
    all_gather x1, waiting for transfers between devices, per_device(): shard_piece = lax.all_gather(packed_v, 'occ', axis=0, tiled=True)  49.2 us
    dot_general x16, matrix products, one_block(): product = jnp.dot(amp_cols, block_part, preferred_element_type=jnp.float32)  43 us
    reshape x16, local copies, waits for them, and re-layouts, one_block(): product.reshape(occ_rows, MAXB, BLK)  30.2 us
    sort x17, other arithmetic, slot_order(): chosen = jnp.argsort(ranking)[:slot_bound]  27.5 us
    select_n x17, other arithmetic, slot_order(): ranking = jnp.where(matching, positions, positions + label_count)  11.5 us
    reduce_sum x16, other arithmetic, one_block(): symmetry = jnp.sum(jnp.where(block_ids == row_start // BLK, k_sym, 0))  11.1 us
  transfers between devices with their start and end apart: 2, of which 2 were waited for; matrix products, arithmetic and copies ran while one was open for 3% of the time, Pallas kernels for 0%

commit v1 on v0

--- a/solution.py
+++ b/solution.py
@@ -53,7 +53,24 @@
         preferred_element_type=jnp.float32,
     )
     packed_v = packed_v.astype(jnp.bfloat16).reshape(shard_rows, MAXB * BLK)
-    shard_piece = lax.all_gather(packed_v, "occ", axis=0, tiled=True)
+    reached, new, n_now = (jax.lax.psum(1, "occ"), jax.lax.axis_index("occ"), packed_v.shape[0])
+    column = [dev_i * reached if c == 0 else dev_i for c, dev_i in enumerate(packed_v.shape)]
+    shard_piece = lax.dynamic_update_slice_in_dim(
+        jnp.zeros(column, packed_v.dtype), packed_v, new * n_now, axis=0
+    )
+    inter = step_out = packed_v
+    for t in range(1, reached // 2 + 1):
+        inter = jax.lax.ppermute(inter, "occ", [(c, (c + 1) % reached) for c in range(reached)])
+        shard_piece = lax.dynamic_update_slice_in_dim(
+            shard_piece, inter, (new - t) % reached * n_now, axis=0
+        )
+        if 2 * t < reached:
+            step_out = jax.lax.ppermute(
+                step_out, "occ", [(c, (c - 1) % reached) for c in range(reached)]
+            )
+            shard_piece = lax.dynamic_update_slice_in_dim(
+                shard_piece, step_out, (new + t) % reached * n_now, axis=0
+            )
     piece_blocks = shard_piece.shape[0] // BLK
 
     def one_block(block_index, running_sum):

time: 405 us -> 359 us (0.89)
  the two profiles are of different devices: /device:TPU:4 before, /device:TPU:1 now
where the time goes in v1:
time: 359 us; the launch traced here: 357 us
  other arithmetic  156 us (43%)
  local copies, waits for them, and re-layouts  64.6 us (18%)
  waiting for transfers between devices  48.8 us (14%)
  matrix products  44.3 us (12%)
  starting transfers between devices  28.3 us (8%)
  between operations  13.7 us (4%)
    scatter-add x16, other arithmetic, one_block(): running_sum.at[:, chosen, :].add(product.reshape(occ_rows, MAXB, BLK))  103 us
    dot_general x16, matrix products, one_block(): product = jnp.dot(amp_cols, block_part, preferred_element_type=jnp.float32)  43.9 us
    all_gather x1, waiting for transfers between devices, per_device(): gathered = lax.all_gather(amplitudes, 'vir', axis=1, tiled=True)  33.4 us
    reshape x16, local copies, waits for them, and re-layouts, one_block(): product.reshape(occ_rows, MAXB, BLK)  30.2 us
    sort x17, other arithmetic, slot_order(): chosen = jnp.argsort(ranking)[:slot_bound]  27.5 us
    ppermute x3, starting transfers between devices, per_device(): jax.lax.ppermute(step_out, 'occ', [(c, (c - 1) % reached) for c in range(...  17.7 us
    ppermute x4, waiting for transfers between devices, per_device(): jax.lax.ppermute(inter, 'occ', [(c, (c + 1) % reached) for c in range(rea...  14.7 us
    select_n x17, other arithmetic, slot_order(): ranking = jnp.where(matching, positions, positions + label_count)  11.5 us
  transfers between devices with their start and end apart: 8, of which 5 were waited for; matrix products, arithmetic and copies ran while one was open for 5% of the time, Pallas kernels for 0%

profile of v1, /device:TPU:1, one launch (start us, length us, event | category | flops | bytes accessed | tf_op | source)
XLA Modules:
  0.0 356.6 jit_solution(6170751198216672941)
XLA Ops:
  10.9 2.5 reshape.82
  16.6 4.9 %collective-permute-start = (bf16[256,640]{0,1:T(8,128)(2,1)S(1)}, bf16[256,640]{0,1:T(8,128)(2,1)S(1)}, u32[]{:S(2)}, u32[]{:S(2)}) collective-permute-start(bf16[256,640]{0,1:T(8,128)(2,1)S(1)} %copy.83), channel_id=1, source_target_pairs={{0,64},{64,128},{128,192},{192,256},{256,320},{320,384},{384,448},... | collective-permute-start | bytes 983048 | tf_op jit(solution)/shard_map/ppermute | solution.py:63
  21.5 8.6 %collective-permute-start.1 = (bf16[256,640]{0,1:T(8,128)(2,1)S(1)}, bf16[256,640]{0,1:T(8,128)(2,1)S(1)}, u32[]{:S(2)}, u32[]{:S(2)}) collective-permute-start(bf16[256,640]{0,1:T(8,128)(2,1)S(1)} %copy.83), channel_id=1, source_target_pairs={{0,448},{64,0},{128,64},{192,128},{256,192},{320,256},{384,320},{4... | collective-permute-start | bytes 983048 | tf_op jit(solution)/shard_map/ppermute | solution.py:68
  30.0 5.5 %collective-permute-done = bf16[256,640]{0,1:T(8,128)(2,1)S(1)} collective-permute-done((bf16[256,640]{0,1:T(8,128)(2,1)S(1)}, bf16[256,640]{0,1:T(8,128)(2,1)S(1)}, u32[]{:S(2)}, u32[]{:S(2)}) %collective-permute-start) | collective-permute-done | bytes 327712 | tf_op jit(solution)/shard_map/ppermute | solution.py:63
  35.5 1.9 collective-permute-start.2
  37.6 4.6 %collective-permute-start.3 = (bf16[256,640]{0,1:T(8,128)(2,1)S(1)}, bf16[256,640]{0,1:T(8,128)(2,1)S(1)}, u32[]{:S(2)}, u32[]{:S(2)}) collective-permute-start(bf16[256,640]{0,1:T(8,128)(2,1)S(1)} %collective-permute-done.1), channel_id=1, source_target_pairs={{0,448},{64,0},{128,64},{192,128},{256,192},{320,256},{384,320},{4... | collective-permute-start | bytes 983048 | tf_op jit(solution)/shard_map/ppermute | solution.py:68
  42.7 3.9 %collective-permute-done.2 = bf16[256,640]{0,1:T(8,128)(2,1)S(1)} collective-permute-done((bf16[256,640]{0,1:T(8,128)(2,1)S(1)}, bf16[256,640]{0,1:T(8,128)(2,1)S(1)}, u32[]{:S(2)}, u32[]{:S(2)}) %collective-permute-start.2) | collective-permute-done | bytes 327712 | tf_op jit(solution)/shard_map/ppermute | solution.py:63
  46.6 1.9 collective-permute-start.4
  49.3 4.6 %collective-permute-start.5 = (bf16[256,640]{0,1:T(8,128)(2,1)S(1)}, bf16[256,640]{0,1:T(8,128)(2,1)S(1)}, u32[]{:S(2)}, u32[]{:S(2)}) collective-permute-start(bf16[256,640]{0,1:T(8,128)(2,1)S(1)} %collective-permute-done.3), channel_id=1, source_target_pairs={{0,448},{64,0},{128,64},{192,128},{256,192},{320,256},{384,320},{4... | collective-permute-start | bytes 983048 | tf_op jit(solution)/shard_map/ppermute | solution.py:68
  56.7 1.9 collective-permute-start.6
  61.4 4.4 %collective-permute-done.6 = bf16[256,640]{0,1:T(8,128)(2,1)S(1)} collective-permute-done((bf16[256,640]{0,1:T(8,128)(2,1)S(1)}, bf16[256,640]{0,1:T(8,128)(2,1)S(1)}, u32[]{:S(2)}, u32[]{:S(2)}) %collective-permute-start.6) | collective-permute-done | bytes 327712 | tf_op jit(solution)/shard_map/ppermute | solution.py:63
  66.7 33.4 %all-gather.2.cloned.1.call-done = bf16[768,2048]{0,1:T(8,128)(2,1)} async-done(((bf16[768,32]{0,1:T(8,128)(2,1)}), bf16[768,2048]{0,1:T(8,128)(2,1)}) %all-gather.2.cloned.1.call-update) | async-done | bytes 3145744 | tf_op jit(solution)/shard_map/all_gather | solution.py:37
  100.2 3.2 copy.64
  103.8 2.4 bitcast_multiply_fusion
  106.2 3.9 %broadcast_in_dim.65 = f32[768,20,128]{2,0,1:T(8,128)} broadcast(f32[]{:T(128)} %constant.138.clone.1), dimensions={} | broadcast | bytes 7864324 | tf_op jit(solution)/shard_map/broadcast_in_dim | solution.py:47
  110.1 226.1 %while.16 = (s32[]{:T(128)}, f32[768,20,128]{2,0,1:T(8,128)}, s32[16]{0:T(128)S(1)}, s32[20]{0:T(128)S(1)}, bf16[768,2048]{1,0:T(8,128)(2,1)}, /*index=5*/bf16[2...) while((s32[]{:T(128)}, f32[768,20,128]{2,0,1:T(8,128)}, ...), condition=%wide.region_6.7_spmd.clone, body=%wide.region_2.6_spmd.clone.sunk | while | flops 126320880 | bytes 12158960 | solution.py:85
  113.2 2.7 fusion.23
  115.9 1.9 copy.90
  117.8 6.5 %scatter_fusion = f32[768,20,128]{2,0,1:T(8,128)} fusion(f32[768,20,128]{2,0,1:T(8,128)} %get-tuple-element.278, s32[5]{0:T(128)S(1)} %compare_select_fusion.8, f32[5,768,128]{2,1,0:T(8,128)S(1)} %bitcast.27), kind=kCustom, calls=%fused_computation.1.clone.clone.1 | custom fusion | flops 491520 | bytes 5898260 | tf_op jit(solution)/shard_map/while/body/eval_jaxpr/scatter-add | solution.py:83
  127.4 2.7 fusion.23
  130.1 1.9 copy.90
  132.0 6.4 %scatter_fusion = f32[768,20,128]{2,0,1:T(8,128)} fusion(f32[768,20,128]{2,0,1:T(8,128)} %get-tuple-element.278, s32[5]{0:T(128)S(1)} %compare_select_fusion.8, f32[5,768,128]{2,1,0:T(8,128)S(1)} %bitcast.27), kind=kCustom, calls=%fused_computation.1.clone.clone.1 | custom fusion | flops 491520 | bytes 5898260 | tf_op jit(solution)/shard_map/while/body/eval_jaxpr/scatter-add | solution.py:83
  141.5 2.7 fusion.23
  144.2 1.9 copy.90
  146.1 6.5 %scatter_fusion = f32[768,20,128]{2,0,1:T(8,128)} fusion(f32[768,20,128]{2,0,1:T(8,128)} %get-tuple-element.278, s32[5]{0:T(128)S(1)} %compare_select_fusion.8, f32[5,768,128]{2,1,0:T(8,128)S(1)} %bitcast.27), kind=kCustom, calls=%fused_computation.1.clone.clone.1 | custom fusion | flops 491520 | bytes 5898260 | tf_op jit(solution)/shard_map/while/body/eval_jaxpr/scatter-add | solution.py:83
  155.7 2.7 fusion.23
  158.4 1.9 copy.90
  160.3 6.4 %scatter_fusion = f32[768,20,128]{2,0,1:T(8,128)} fusion(f32[768,20,128]{2,0,1:T(8,128)} %get-tuple-element.278, s32[5]{0:T(128)S(1)} %compare_select_fusion.8, f32[5,768,128]{2,1,0:T(8,128)S(1)} %bitcast.27), kind=kCustom, calls=%fused_computation.1.clone.clone.1 | custom fusion | flops 491520 | bytes 5898260 | tf_op jit(solution)/shard_map/while/body/eval_jaxpr/scatter-add | solution.py:83
  169.8 2.7 fusion.23
  172.5 1.9 copy.90
  174.4 6.4 %scatter_fusion = f32[768,20,128]{2,0,1:T(8,128)} fusion(f32[768,20,128]{2,0,1:T(8,128)} %get-tuple-element.278, s32[5]{0:T(128)S(1)} %compare_select_fusion.8, f32[5,768,128]{2,1,0:T(8,128)S(1)} %bitcast.27), kind=kCustom, calls=%fused_computation.1.clone.clone.1 | custom fusion | flops 491520 | bytes 5898260 | tf_op jit(solution)/shard_map/while/body/eval_jaxpr/scatter-add | solution.py:83
  183.9 2.7 fusion.23
  186.7 1.9 copy.90
  188.6 6.4 %scatter_fusion = f32[768,20,128]{2,0,1:T(8,128)} fusion(f32[768,20,128]{2,0,1:T(8,128)} %get-tuple-element.278, s32[5]{0:T(128)S(1)} %compare_select_fusion.8, f32[5,768,128]{2,1,0:T(8,128)S(1)} %bitcast.27), kind=kCustom, calls=%fused_computation.1.clone.clone.1 | custom fusion | flops 491520 | bytes 5898260 | tf_op jit(solution)/shard_map/while/body/eval_jaxpr/scatter-add | solution.py:83
  198.1 2.7 fusion.23
  200.8 1.9 copy.90
  202.7 6.4 %scatter_fusion = f32[768,20,128]{2,0,1:T(8,128)} fusion(f32[768,20,128]{2,0,1:T(8,128)} %get-tuple-element.278, s32[5]{0:T(128)S(1)} %compare_select_fusion.8, f32[5,768,128]{2,1,0:T(8,128)S(1)} %bitcast.27), kind=kCustom, calls=%fused_computation.1.clone.clone.1 | custom fusion | flops 491520 | bytes 5898260 | tf_op jit(solution)/shard_map/while/body/eval_jaxpr/scatter-add | solution.py:83
  212.2 2.7 fusion.23
  214.9 1.9 copy.90
  216.8 6.4 %scatter_fusion = f32[768,20,128]{2,0,1:T(8,128)} fusion(f32[768,20,128]{2,0,1:T(8,128)} %get-tuple-element.278, s32[5]{0:T(128)S(1)} %compare_select_fusion.8, f32[5,768,128]{2,1,0:T(8,128)S(1)} %bitcast.27), kind=kCustom, calls=%fused_computation.1.clone.clone.1 | custom fusion | flops 491520 | bytes 5898260 | tf_op jit(solution)/shard_map/while/body/eval_jaxpr/scatter-add | solution.py:83
  226.3 2.7 fusion.23
  229.0 1.9 copy.90
  230.9 6.4 %scatter_fusion = f32[768,20,128]{2,0,1:T(8,128)} fusion(f32[768,20,128]{2,0,1:T(8,128)} %get-tuple-element.278, s32[5]{0:T(128)S(1)} %compare_select_fusion.8, f32[5,768,128]{2,1,0:T(8,128)S(1)} %bitcast.27), kind=kCustom, calls=%fused_computation.1.clone.clone.1 | custom fusion | flops 491520 | bytes 5898260 | tf_op jit(solution)/shard_map/while/body/eval_jaxpr/scatter-add | solution.py:83
  240.4 2.7 fusion.23
  243.2 1.9 copy.90
  245.1 6.4 %scatter_fusion = f32[768,20,128]{2,0,1:T(8,128)} fusion(f32[768,20,128]{2,0,1:T(8,128)} %get-tuple-element.278, s32[5]{0:T(128)S(1)} %compare_select_fusion.8, f32[5,768,128]{2,1,0:T(8,128)S(1)} %bitcast.27), kind=kCustom, calls=%fused_computation.1.clone.clone.1 | custom fusion | flops 491520 | bytes 5898260 | tf_op jit(solution)/shard_map/while/body/eval_jaxpr/scatter-add | solution.py:83
  254.5 2.7 fusion.23
  257.3 1.9 copy.90
  259.2 6.4 %scatter_fusion = f32[768,20,128]{2,0,1:T(8,128)} fusion(f32[768,20,128]{2,0,1:T(8,128)} %get-tuple-element.278, s32[5]{0:T(128)S(1)} %compare_select_fusion.8, f32[5,768,128]{2,1,0:T(8,128)S(1)} %bitcast.27), kind=kCustom, calls=%fused_computation.1.clone.clone.1 | custom fusion | flops 491520 | bytes 5898260 | tf_op jit(solution)/shard_map/while/body/eval_jaxpr/scatter-add | solution.py:83
  268.7 2.7 fusion.23
  273.3 6.4 %scatter_fusion = f32[768,20,128]{2,0,1:T(8,128)} fusion(f32[768,20,128]{2,0,1:T(8,128)} %get-tuple-element.278, s32[5]{0:T(128)S(1)} %compare_select_fusion.8, f32[5,768,128]{2,1,0:T(8,128)S(1)} %bitcast.27), kind=kCustom, calls=%fused_computation.1.clone.clone.1 | custom fusion | flops 491520 | bytes 5898260 | tf_op jit(solution)/shard_map/while/body/eval_jaxpr/scatter-add | solution.py:83
  282.8 2.7 fusion.23
  285.5 1.9 copy.90
  287.4 6.4 %scatter_fusion = f32[768,20,128]{2,0,1:T(8,128)} fusion(f32[768,20,128]{2,0,1:T(8,128)} %get-tuple-element.278, s32[5]{0:T(128)S(1)} %compare_select_fusion.8, f32[5,768,128]{2,1,0:T(8,128)S(1)} %bitcast.27), kind=kCustom, calls=%fused_computation.1.clone.clone.1 | custom fusion | flops 491520 | bytes 5898260 | tf_op jit(solution)/shard_map/while/body/eval_jaxpr/scatter-add | solution.py:83
  296.9 2.7 fusion.23
  299.6 1.9 copy.90
  301.5 6.5 %scatter_fusion = f32[768,20,128]{2,0,1:T(8,128)} fusion(f32[768,20,128]{2,0,1:T(8,128)} %get-tuple-element.278, s32[5]{0:T(128)S(1)} %compare_select_fusion.8, f32[5,768,128]{2,1,0:T(8,128)S(1)} %bitcast.27), kind=kCustom, calls=%fused_computation.1.clone.clone.1 | custom fusion | flops 491520 | bytes 5898260 | tf_op jit(solution)/shard_map/while/body/eval_jaxpr/scatter-add | solution.py:83
  311.1 2.7 fusion.23
  313.8 1.9 copy.90
  315.7 6.4 %scatter_fusion = f32[768,20,128]{2,0,1:T(8,128)} fusion(f32[768,20,128]{2,0,1:T(8,128)} %get-tuple-element.278, s32[5]{0:T(128)S(1)} %compare_select_fusion.8, f32[5,768,128]{2,1,0:T(8,128)S(1)} %bitcast.27), kind=kCustom, calls=%fused_computation.1.clone.clone.1 | custom fusion | flops 491520 | bytes 5898260 | tf_op jit(solution)/shard_map/while/body/eval_jaxpr/scatter-add | solution.py:83
  325.2 2.7 fusion.23
  329.8 6.4 %scatter_fusion = f32[768,20,128]{2,0,1:T(8,128)} fusion(f32[768,20,128]{2,0,1:T(8,128)} %get-tuple-element.278, s32[5]{0:T(128)S(1)} %compare_select_fusion.8, f32[5,768,128]{2,1,0:T(8,128)S(1)} %bitcast.27), kind=kCustom, calls=%fused_computation.1.clone.clone.1 | custom fusion | flops 491520 | bytes 5898260 | tf_op jit(solution)/shard_map/while/body/eval_jaxpr/scatter-add | solution.py:83
  336.3 7.2 %copy.79 = bf16[768,20,128]{0,2,1:T(8,128)(2,1)} copy(f32[768,20,128]{2,0,1:T(8,128)} %get-tuple-element.185) | data formatting | bytes 11796480 | tf_op jit(solution)/shard_map/while | solution.py:85
  343.4 6.3 %copy.80 = bf16[768,2560]{1,0:T(8,128)(2,1)} copy(bf16[768,2560]{0,1:T(8,128)(2,1)} %bitcast.29) | data formatting | bytes 7864320 | tf_op jit(solution)/shard_map/convert_element_type | solution.py:86
  (128 shorter events, 68.2 us)
Async XLA Ops:
  6.5 93.6 %all-gather.2.cloned.1.call-start = ((), (), s32[]{:S(2)}) async-start(), calls=%async_computation | async-start | bytes 3194880 | tf_op jit(solution)/shard_map/all_gather | solution.py:37
  13.8 28.3 %copy-start = (s32[6]{0:T(128)S(1)}, s32[6]{0:T(128)}, u32[]{:S(2)}) copy-start(s32[6]{0:T(128)} %param.9) | copy-start | bytes 76
  13.9 28.3 %copy-start.1 = (s32[16]{0:T(128)S(1)}, s32[16]{0:T(128)}, u32[]{:S(2)}) copy-start(s32[16]{0:T(128)} %param.11) | copy-start | bytes 196
  16.6 18.9 %collective-permute-start = (bf16[256,640]{0,1:T(8,128)(2,1)S(1)}, bf16[256,640]{0,1:T(8,128)(2,1)S(1)}, u32[]{:S(2)}, u32[]{:S(2)}) collective-permute-start(bf16[256,640]{0,1:T(8,128)(2,1)S(1)} %copy.83), channel_id=1, source_target_pairs={{0,64},{64,128},{128,192},{192,256},{256,320},{320,384},{384,448},... | collective-permute-start | bytes 983048 | tf_op jit(solution)/shard_map/ppermute | solution.py:63
  21.5 16.1 %collective-permute-start.1 = (bf16[256,640]{0,1:T(8,128)(2,1)S(1)}, bf16[256,640]{0,1:T(8,128)(2,1)S(1)}, u32[]{:S(2)}, u32[]{:S(2)}) collective-permute-start(bf16[256,640]{0,1:T(8,128)(2,1)S(1)} %copy.83), channel_id=1, source_target_pairs={{0,448},{64,0},{128,64},{192,128},{256,192},{320,256},{384,320},{4... | collective-permute-start | bytes 983048 | tf_op jit(solution)/shard_map/ppermute | solution.py:68
  35.5 11.1 %collective-permute-start.2 = (bf16[256,640]{0,1:T(8,128)(2,1)S(1)}, bf16[256,640]{0,1:T(8,128)(2,1)S(1)}, u32[]{:S(2)}, u32[]{:S(2)}) collective-permute-start(bf16[256,640]{0,1:T(8,128)(2,1)S(1)} %collective-permute-done), channel_id=1, source_target_pairs={{0,64},{64,128},{128,192},{192,256},{256,320},{320,384},{384,448},... | collective-permute-start | bytes 983048 | tf_op jit(solution)/shard_map/ppermute | solution.py:63
  37.6 11.7 %collective-permute-start.3 = (bf16[256,640]{0,1:T(8,128)(2,1)S(1)}, bf16[256,640]{0,1:T(8,128)(2,1)S(1)}, u32[]{:S(2)}, u32[]{:S(2)}) collective-permute-start(bf16[256,640]{0,1:T(8,128)(2,1)S(1)} %collective-permute-done.1), channel_id=1, source_target_pairs={{0,448},{64,0},{128,64},{192,128},{256,192},{320,256},{384,320},{4... | collective-permute-start | bytes 983048 | tf_op jit(solution)/shard_map/ppermute | solution.py:68
  46.6 10.1 %collective-permute-start.4 = (bf16[256,640]{0,1:T(8,128)(2,1)S(1)}, bf16[256,640]{0,1:T(8,128)(2,1)S(1)}, u32[]{:S(2)}, u32[]{:S(2)}) collective-permute-start(bf16[256,640]{0,1:T(8,128)(2,1)S(1)} %collective-permute-done.2), channel_id=1, source_target_pairs={{0,64},{64,128},{128,192},{192,256},{256,320},{320,384},{384,448},... | collective-permute-start | bytes 983048 | tf_op jit(solution)/shard_map/ppermute | solution.py:63
  49.3 10.4 %collective-permute-start.5 = (bf16[256,640]{0,1:T(8,128)(2,1)S(1)}, bf16[256,640]{0,1:T(8,128)(2,1)S(1)}, u32[]{:S(2)}, u32[]{:S(2)}) collective-permute-start(bf16[256,640]{0,1:T(8,128)(2,1)S(1)} %collective-permute-done.3), channel_id=1, source_target_pairs={{0,448},{64,0},{128,64},{192,128},{256,192},{320,256},{384,320},{4... | collective-permute-start | bytes 983048 | tf_op jit(solution)/shard_map/ppermute | solution.py:68
  56.7 9.0 %collective-permute-start.6 = (bf16[256,640]{0,1:T(8,128)(2,1)S(1)}, bf16[256,640]{0,1:T(8,128)(2,1)S(1)}, u32[]{:S(2)}, u32[]{:S(2)}) collective-permute-start(bf16[256,640]{0,1:T(8,128)(2,1)S(1)} %collective-permute-done.4), channel_id=1, source_target_pairs={{0,64},{64,128},{128,192},{192,256},{256,320},{320,384},{384,448},... | collective-permute-start | bytes 983048 | tf_op jit(solution)/shard_map/ppermute | solution.py:63
  106.2 3.9 %copy-start.2 = (s32[20]{0:T(128)S(1)}, s32[20]{0:T(128)}, u32[]{:S(2)}) copy-start(s32[20]{0:T(128)} %param.10) | copy-start | bytes 244
Sparse Core Ops, SparseCore 0:
  10.7 89.4 all-gather.1
